TPU v7x, 512 devices: a whole 4x4x16 slice. The times are simulated.
512 devices in a mesh: grp: 32 (over z_hi, x, core), dev: 16 (over z_lo, y).
Axes of the slice: x: 4, y: 4, z: 16 (z_hi: 4, z_lo: 4; z = z_hi * 4 + z_lo), core: 2. Of those that a mesh axis runs over, the one named last changes fastest.
Arguments:
- row_ptr: int32 [32, 65], P('grp'), may hold values from 0 to 2048, as said below
- col_off: int32 [32, 2048], P('grp', 'dev'), may hold values from -32 to 32, as said below
- blocks: bfloat16 [65536, 128, 128], P(('grp', 'dev')), may hold values from -0.09375 to 0.09375
- trial: bfloat16 [262144, 256], P(('grp', 'dev')), may hold values from -6 to 6
Outputs:
- filtered: bfloat16 [393216, 256], P(('grp', 'dev'))
Inputs may be any that keep to these rules, and one draw needn't show every extreme that they name: row_ptr[g, 0] = 0 and row_ptr[g, 64] = 2048; every block row holds 24 to 48 nonzero blocks, both reached; in every band the 128 nonzero blocks of some device hold the last blocks of 6 rows. For every device d of a band, the block row that holds nonzero block d * 128 lies between (d - 1) * 4 and (d + 1) * 4. `col_off`: the offsets of one block row are distinct, increasing, and include -32, 0 and 32.
All inputs are finite; a program needn't handle non-finite values.
Results may differ from a plain program's by a relative error of at most 0.0095.
Values may be sent and summed in bfloat16 or wider, within the bound.
No kernel may reach another device: no remote copies, remote signals or barrier semaphores. Data moves between devices by JAX's collectives and lax.ppermute only.
A program may use at most 64 MiB of HBM per device.

v0:
```python
import jax
import jax.numpy as jnp
from jax import lax
from jax.experimental import pallas as pl
from jax.experimental.pallas import tpu as pltpu
from jax.sharding import PartitionSpec as P


BLK = 128
VEC = 256
SPAN = 6
HOME = 4
NNZ = 128
ROWS = 64
DEPTH = 4
HALF = 32
WIN = ROWS + 2 * HALF
DEVICES = 512
CENTER = 0.5
INV = 1.0 / 1.5
BF = jnp.bfloat16
F32 = jnp.float32
AXES = ("grp", "dev")


def swap_z(odd):
    pairs = []
    for g in range(DEVICES):
        group = g // 4
        other = group + 1 if group % 2 == odd else group - 1
        pairs.append((g, (other * 4 + g % 4) % DEVICES))
    return pairs


def swap_y(odd):
    return [(g, g // 4 * 4 + (3 - g % 4 if odd else (g % 4) ^ 1)) for g in range(DEVICES)]


def shift_dev(step):
    return [(g, g + step) for g in range(DEVICES) if 0 <= g % 16 + step < 16]


def swap_dev(odd):
    pairs = []
    for g in range(DEVICES):
        other = g + 1 if g % 2 == odd else g - 1
        if other // 16 == g // 16:
            pairs.append((g, other))
    return pairs


def edge_rows():
    down = [(g, (g + 9) % DEVICES) for g in range(DEVICES) if g % 4 == 3]
    up = [(g, (g - 9) % DEVICES) for g in range(DEVICES) if g % 4 == 0]
    return down + up + [(g, (g - 11) % DEVICES) for g in range(DEVICES) if g % 4 == 1]


def send(value, pairs):
    return lax.ppermute(value, AXES, pairs)


def gather_arrays(shard, member, held_back):
    side = 1 - 2 * (member // 4 % 2)
    lower = member % 4 < 2
    next_a = send(shard, swap_z(0))
    next_b = send(shard, swap_z(1))
    edge = send(shard, edge_rows())
    first = jnp.stack([shard, next_a])
    far_b = send(next_a, swap_z(1))
    far_a = send(next_b, swap_z(0))
    first_a = send(first, swap_y(0))
    first_b = send(first, swap_y(1))
    first_x = send(first_a, swap_y(1))
    second_a = send(next_b, swap_y(0))
    second_b = send(next_b, swap_y(1))
    second_x = send(second_b, swap_y(0))
    third = jnp.stack([far_a, far_b])
    third_a = send(third, swap_y(0))
    third_b = send(third, swap_y(1))
    wants_far_b = lower == (side == 1)
    wanted = jnp.where(wants_far_b, third_b[1], third_b[0])
    other = jnp.where(wants_far_b, third_b[0, :1], third_b[1, :1])
    last = send(jnp.concatenate([wanted, jnp.where(lower, other, edge[:1])]), swap_y(0))
    arrays = [first, first_a, first_b, first_x]
    arrays += [next_b, second_a, second_b, second_x, third, third_a, third_b, last, edge]
    arrays = [array.reshape(-1, BLK, VEC) for array in arrays]
    if held_back is None:
        return arrays, None
    return arrays, lax.optimization_barrier((held_back, first))[0]


def window_pieces(member):
    zl = member >> 2
    y = member & 3
    side = 1 - 2 * (zl & 1)

    def at(offset, source):
        return (8 + (zl + offset) * 4 + source) * HOME

    pieces = []
    for array, source in enumerate((y, y ^ 1, 3 - y, y ^ 2)):
        pieces += [(array, 4 * i, HOME, at(offset, source)) for i, offset in enumerate((0, side))]
        pieces.append((4 + array, 0, HOME, at(-side, source)))
    for array, source in enumerate((y, y ^ 1, 3 - y)):
        offsets = (2 * side, -2 * side)
        pieces += [(8 + array, 4 * i, HOME, at(offset, source)) for i, offset in enumerate(offsets)]
    lower = y < 2
    pieces.append((11, 0, HOME, at(jnp.where(lower, -2, 2), y ^ 2)))
    single = jnp.where(lower, at(2, y ^ 2), at(3, y - 2))
    pieces.append((11, HOME, 1, jnp.where(single < WIN, single, -1)))
    whole = jnp.where(y == 0, at(-3, 3), jnp.where(y == 3, at(3, 0), -1))
    pieces.append((12, 0, HOME, jnp.where(whole < WIN, whole, -1)))
    return pieces


def fetch(blocks):
    def kernel(source, target, sem):
        copy = pltpu.make_async_copy(source, target, sem.at[0])
        copy.start()
        copy.wait()

    return pl.pallas_call(
        kernel,
        out_shape=pltpu.VMEM(blocks.shape, blocks.dtype),
        in_specs=[pl.BlockSpec(memory_space=pltpu.HBM)],
        out_specs=pl.BlockSpec(memory_space=pltpu.VMEM),
        scratch_shapes=[pltpu.SemaphoreType.DMA((1,))],
        compiler_params=pltpu.CompilerParams(vmem_limit_bytes=1024 * 1024),
    )(blocks)


def block_products(pointer, offsets, member, homed, held, arrays, window, total, copy_sem):
    loads = []
    for which, (array, entry, rows, start) in enumerate(window_pieces(member)):
        copy = pltpu.make_async_copy(
            arrays[array].at[pl.ds(entry, rows)],
            window.at[pl.ds(jnp.maximum(start, 0), rows)],
            copy_sem.at[which],
        )
        loads.append((start, copy))
        pl.when(start >= 0)(copy.start)
    total[...] = jnp.zeros(total.shape, F32)
    first_nnz = member * NNZ
    first_row = jnp.int32(0)
    for r in range(ROWS):
        first_row += (pointer[0, r + 1] <= first_nnz).astype(jnp.int32)
    shift = first_row - (HOME * member - HOME) if homed else 0
    finished = jnp.int32(0)
    for r in range(SPAN + 1):
        end = pointer[0, jnp.minimum(first_row + r + 1, ROWS)]
        ends_here = jnp.logical_and(first_row + r < ROWS, end <= first_nnz + NNZ)
        finished += ends_here.astype(jnp.int32)
    for start, copy in loads:
        pl.when(start >= 0)(copy.wait)

    def one_row(r, carry):
        row = first_row + r
        low = jnp.clip(pointer[0, jnp.minimum(row, ROWS)] - first_nnz, 0, NNZ)
        high = jnp.clip(pointer[0, jnp.minimum(row + 1, ROWS)] - first_nnz, 0, NNZ)

        def one_group(q, value):
            base = low + q * DEPTH
            lefts = []
            rights = []
            for i in range(DEPTH):
                p = base + i
                inside = jnp.minimum(p, high - 1)
                block = held[inside]
                lefts.append(block if i == 0 else jnp.where(p < high, block, jnp.zeros_like(block)))
                rights.append(window[row + offsets[0, inside] + HALF])
            left = jnp.concatenate(lefts, axis=1)
            right = jnp.concatenate(rights, axis=0)
            return value + jnp.dot(left, right, preferred_element_type=F32)

        total[shift + r] = lax.fori_loop(
            0, (high - low + DEPTH - 1) // DEPTH, one_group, jnp.zeros((BLK, VEC), F32)
        )
        return carry

    lax.fori_loop(0, SPAN + 1, one_row, 0)
    return first_row, finished


def call_products(body, homed, scalars, held, arrays, extra, outs, touched):
    count = len(arrays)

    def kernel(*refs):
        pointer, offsets, place, held_ref = refs[:4]
        array_refs = refs[4 : 4 + count]
        extra_refs = refs[4 + count : 4 + count + len(extra)]
        out_refs = refs[4 + count + len(extra) : 4 + count + len(extra) + len(outs)]
        window, total, copy_sem = refs[4 + count + len(extra) + len(outs) :]
        member = place[0]
        first_row, finished = block_products(
            pointer, offsets, member, homed, held_ref, array_refs, window, total, copy_sem
        )
        body(member, first_row, finished, window, total, extra_refs, out_refs)

    hbm = pl.BlockSpec(memory_space=pltpu.HBM)
    vmem = pl.BlockSpec(memory_space=pltpu.VMEM)
    smem = pl.BlockSpec(memory_space=pltpu.SMEM)
    return pl.pallas_call(
        kernel,
        out_shape=outs,
        in_specs=[smem] * 3 + [vmem] + [hbm] * count + [vmem] * len(extra),
        out_specs=[vmem] * len(outs),
        scratch_shapes=[
            pltpu.VMEM((WIN, BLK, VEC), BF),
            pltpu.VMEM((touched, BLK, VEC), F32),
            pltpu.SemaphoreType.DMA((len(window_pieces(0)),)),
        ],
        compiler_params=pltpu.CompilerParams(vmem_limit_bytes=40 * 1024 * 1024),
    )(*scalars, held, *arrays, *extra)


def body_first(member, first, finished, window, total, extra, outs):
    to_pair, own, to_next, over, older = outs
    even = (member & 1) == 0
    to_pair[...] = total[pl.ds(jnp.where(even, 8, 0), HOME)].astype(BF)
    own[...] = total[4:8]
    to_next[...] = total[pl.ds(jnp.where(even, 0, 8), HOME)].astype(BF)
    over[...] = total[12:13].astype(BF)
    for s in range(SPAN):
        older[s] = window[first + HALF + s]


def body_second(member, first, finished, window, total, extra, outs):
    (older,) = extra
    done, tail, head = outs
    for s in range(SPAN):
        present = window[first + HALF + s].astype(F32)
        value = 2.0 * (total[s] - CENTER * present) * INV - older[s].astype(F32)
        value = jnp.where(s < finished, value, 0.0)
        done[s] = value.astype(BF)
        if s == 0:
            head[...] = value
    tail[...] = total[jnp.minimum(finished, SPAN)].astype(BF)


def local(row_ptr, col_off, blocks, trial):
    member = lax.axis_index("dev")
    scalars = (row_ptr, col_off, member[None].astype(jnp.int32))
    shard = trial.reshape(HOME, BLK, VEC)

    shape = jax.ShapeDtypeStruct
    arrays, blocks = gather_arrays(shard, member, blocks)
    held = fetch(blocks)
    to_pair, own, to_next, over, older = call_products(
        body_first,
        True,
        scalars,
        held,
        arrays,
        [],
        [
            shape((4, BLK, VEC), BF),
            shape((4, BLK, VEC), F32),
            shape((4, BLK, VEC), BF),
            shape((1, BLK, VEC), BF),
            shape((SPAN, BLK, VEC), BF),
        ],
        15,
    )
    over = send(over, shift_dev(2))
    by_pair = send(to_pair, swap_dev(0))
    by_next = send(to_next, swap_dev(1))
    sums = own + by_pair.astype(F32) + by_next.astype(F32)
    sums = sums.at[:1].add(over.astype(F32))
    updated = ((sums - CENTER * shard.astype(F32)) / 1.5).astype(BF)

    arrays, _ = gather_arrays(updated, member, None)
    done, tail, head = call_products(
        body_second,
        False,
        scalars,
        held,
        arrays,
        [older],
        [shape((SPAN, BLK, VEC), BF), shape((BLK, VEC), BF), shape((BLK, VEC), F32)],
        7,
    )
    carried = send(tail, shift_dev(1)).astype(F32)
    top = head + 2.0 * carried * INV
    done = done.at[0].set(top.astype(BF))
    return done.reshape(SPAN * BLK, VEC)


def solution(mesh):
    in_specs = (
        P("grp", None),
        P("grp", "dev"),
        P(("grp", "dev"), None, None),
        P(("grp", "dev"), None),
    )
    out_specs = P(("grp", "dev"), None)
    return jax.shard_map(local, mesh=mesh, in_specs=in_specs, out_specs=out_specs, check_vma=False)
```

profile of v0, /device:TPU:70, one launch (start us, length us, event | category | flops | bytes accessed | tf_op | source)
XLA Modules:
  0.0 219.9 jit_solution(1655731522983703476)
XLA Ops:
  5.8 10.0 %collective-permute-done.4.refs_8_ = bf16[4,128,256]{2,1,0:T(8,128)(2,1)S(1)} collective-permute-done((bf16[4,128,256]{2,1,0:T(8,128)(2,1)}, bf16[4,128,256]{2,1,0:T(8,128)(2,1)S(1)}, u32[]{:S(2)}, u32[]{:S(2)}) %collective-permute-start.4) | collective-permute-done | bytes 262176 | tf_op jit(solution)/shard_map/ppermute | solution.py:59
  24.8 8.8 %collective-permute-done.9 = bf16[4,128,256]{2,1,0:T(8,128)(2,1)S(1)} collective-permute-done((bf16[4,128,256]{2,1,0:T(8,128)(2,1)S(1)}, bf16[4,128,256]{2,1,0:T(8,128)(2,1)S(1)}, u32[]{:S(2)}, u32[]{:S(2)}) %collective-permute-start.9) | collective-permute-done | bytes 262176 | tf_op jit(solution)/shard_map/ppermute | solution.py:59
  33.7 4.9 %collective-permute-start.11 = (bf16[2,4,128,256]{3,2,1,0:T(8,128)(2,1)S(1)}, bf16[2,4,128,256]{3,2,1,0:T(8,128)(2,1)S(1)}, u32[]{:S(2)}, u32[]{:S(2)}) collective-permute-start(bf16[2,4,128,256]{3,2,1,0:T(8,128)(2,1)S(1)} %pad_maximum_fusion.1), channel_id=1, source_target_pairs={{0,3},{1,2},{2,1},{3,0},{4,7},{5,6},{6,5},{7,4},{8,11},{9,10},{10,... | collective-permute-start | bytes 1572872 | tf_op jit(solution)/shard_map/ppermute | solution.py:59
  46.6 4.1 %collective-permute-start.6 = (bf16[4,128,256]{2,1,0:T(8,128)(2,1)S(1)}, bf16[4,128,256]{2,1,0:T(8,128)(2,1)S(1)}, u32[]{:S(2)}, u32[]{:S(2)}) collective-permute-start(bf16[4,128,256]{2,1,0:T(8,128)(2,1)S(1)} %collective-permute-done.4.refs_8_), channel_id=1, source_target_pairs={{0,3},{1,2},{2,1},{3,0},{4,7},{5,6},{6,5},{7,4},{8,11},{9,10},{10,... | collective-permute-start | bytes 786440 | tf_op jit(solution)/shard_map/ppermute | solution.py:59
  50.7 6.5 %collective-permute-done.11 = bf16[2,4,128,256]{3,2,1,0:T(8,128)(2,1)S(1)} collective-permute-done((bf16[2,4,128,256]{3,2,1,0:T(8,128)(2,1)S(1)}, bf16[2,4,128,256]{3,2,1,0:T(8,128)(2,1)S(1)}, u32[]{:S(2)}, u32[]{:S(2)}) %collective-permute-start.11) | collective-permute-done | bytes 524320 | tf_op jit(solution)/shard_map/ppermute | solution.py:59
  59.1 3.9 %collective-permute-start.10 = (bf16[2,4,128,256]{3,2,1,0:T(8,128)(2,1)S(1)}, bf16[2,4,128,256]{3,2,1,0:T(8,128)(2,1)S(1)}, u32[]{:S(2)}, u32[]{:S(2)}) collective-permute-start(bf16[2,4,128,256]{3,2,1,0:T(8,128)(2,1)S(1)} %pad_maximum_fusion.1), channel_id=1, source_target_pairs={{0,1},{1,0},{2,3},{3,2},{4,5},{5,4},{6,7},{7,6},{8,9},{9,8},{10,11... | collective-permute-start | bytes 1572872 | tf_op jit(solution)/shard_map/ppermute | solution.py:59
  65.1 8.9 %collective-permute-done.6.refs_10_ = bf16[4,128,256]{2,1,0:T(8,128)(2,1)S(1)} collective-permute-done((bf16[4,128,256]{2,1,0:T(8,128)(2,1)S(1)}, bf16[4,128,256]{2,1,0:T(8,128)(2,1)S(1)}, u32[]{:S(2)}, u32[]{:S(2)}) %collective-permute-start.6) | collective-permute-done | bytes 262176 | tf_op jit(solution)/shard_map/ppermute | solution.py:59
  75.9 3.9 %collective-permute-start.7 = (bf16[4,128,256]{2,1,0:T(8,128)(2,1)S(1)}, bf16[4,128,256]{2,1,0:T(8,128)(2,1)S(1)}, u32[]{:S(2)}, u32[]{:S(2)}) collective-permute-start(bf16[4,128,256]{2,1,0:T(8,128)(2,1)S(1)} %collective-permute-done.6.refs_10_), channel_id=1, source_target_pairs={{0,1},{1,0},{2,3},{3,2},{4,5},{5,4},{6,7},{7,6},{8,9},{9,8},{10,11... | collective-permute-start | bytes 786440 | tf_op jit(solution)/shard_map/ppermute | solution.py:59
  82.3 7.8 %collective-permute-done.7.refs_11_ = bf16[4,128,256]{2,1,0:T(8,128)(2,1)S(1)} collective-permute-done((bf16[4,128,256]{2,1,0:T(8,128)(2,1)S(1)}, bf16[4,128,256]{2,1,0:T(8,128)(2,1)S(1)}, u32[]{:S(2)}, u32[]{:S(2)}) %collective-permute-start.7) | collective-permute-done | bytes 262176 | tf_op jit(solution)/shard_map/ppermute | solution.py:59
  90.2 8.3 %shard_map.47 = (bf16[4,128,256]{2,1,0:T(8,128)(2,1)S(1)}, f32[4,128,256]{2,1,0:T(8,128)S(1)}, bf16[4,128,256]{2,1,0:T(8,128)(2,1)S(1)}, bf16[1,128,256]{2,1,0:T(8,128)(2,1)S(1)}, bf16[6,128,256]{2,1,0:T(8,128)(2,1)S(1)}) custom-call(s32[1,65]{1,0:T(1,128)S(1)} %copy-done.1, s32[1,128]{1,0:T(1,128)S(1)} %copy-done.2, s32[1]{0:T(128)} %bitcast.refs_2_, ...), custom_call_target="tpu_custom_call" | custom-call | tf_op jit(solution)/shard_map/pallas_call | solution.py:202
  102.7 5.7 %collective-permute-start.16 = (bf16[1,128,256]{2,1,0:T(8,128)(2,1)S(1)}, bf16[1,128,256]{2,1,0:T(8,128)(2,1)S(1)}, u32[]{:S(2)}, u32[]{:S(2)}) collective-permute-start(bf16[1,128,256]{2,1,0:T(8,128)(2,1)S(1)} %get-tuple-element.42), channel_id=1, source_target_pairs={{0,2},{1,3},{2,4},{3,5},{4,6},{5,7},{6,8},{7,9},{8,10},{9,11},{10,... | collective-permute-start | bytes 196616 | tf_op jit(solution)/shard_map/ppermute | solution.py:59
  108.4 4.5 %collective-permute-done.15 = bf16[4,128,256]{2,1,0:T(8,128)(2,1)S(1)} collective-permute-done((bf16[4,128,256]{2,1,0:T(8,128)(2,1)S(1)}, bf16[4,128,256]{2,1,0:T(8,128)(2,1)S(1)}, u32[]{:S(2)}, u32[]{:S(2)}) %collective-permute-start.15) | collective-permute-done | bytes 262176 | tf_op jit(solution)/shard_map/ppermute | solution.py:59
  115.1 5.5 %collective-permute-start.17 = (bf16[4,128,256]{2,1,0:T(8,128)(2,1)S(1)}, bf16[4,128,256]{2,1,0:T(8,128)(2,1)S(1)}, u32[]{:S(2)}, u32[]{:S(2)}) collective-permute-start(bf16[4,128,256]{2,1,0:T(8,128)(2,1)S(1)} %multiply_convert_fusion), channel_id=1, source_target_pairs={{0,4},{1,5},{2,6},{3,7},{4,0},{5,1},{6,2},{7,3},{8,12},{9,13},{10,... | collective-permute-start | bytes 786440 | tf_op jit(solution)/shard_map/ppermute | solution.py:59
  123.7 7.1 %collective-permute-start.25 = (bf16[4,128,256]{2,1,0:T(8,128)(2,1)S(1)}, bf16[4,128,256]{2,1,0:T(8,128)(2,1)S(1)}, u32[]{:S(2)}, u32[]{:S(2)}) collective-permute-start(bf16[4,128,256]{2,1,0:T(8,128)(2,1)S(1)} %collective-permute-done.21.refs_8_), channel_id=1, source_target_pairs={{0,4},{1,5},{2,6},{3,7},{4,0},{5,1},{6,2},{7,3},{8,12},{9,13},{10,... | collective-permute-start | bytes 786440 | tf_op jit(solution)/shard_map/ppermute | solution.py:59
  132.7 3.9 %collective-permute-done.25 = bf16[4,128,256]{2,1,0:T(8,128)(2,1)S(1)} collective-permute-done((bf16[4,128,256]{2,1,0:T(8,128)(2,1)S(1)}, bf16[4,128,256]{2,1,0:T(8,128)(2,1)S(1)}, u32[]{:S(2)}, u32[]{:S(2)}) %collective-permute-start.25) | collective-permute-done | bytes 262176 | tf_op jit(solution)/shard_map/ppermute | solution.py:59
  136.6 9.4 %collective-permute-done.26 = bf16[4,128,256]{2,1,0:T(8,128)(2,1)S(1)} collective-permute-done((bf16[4,128,256]{2,1,0:T(8,128)(2,1)S(1)}, bf16[4,128,256]{2,1,0:T(8,128)(2,1)S(1)}, u32[]{:S(2)}, u32[]{:S(2)}) %collective-permute-start.26) | collective-permute-done | bytes 262176 | tf_op jit(solution)/shard_map/ppermute | solution.py:59
  152.8 4.4 %collective-permute-start.19 = (bf16[2,4,128,256]{3,2,1,0:T(8,128)(2,1)S(1)}, bf16[2,4,128,256]{3,2,1,0:T(8,128)(2,1)S(1)}, u32[]{:S(2)}, u32[]{:S(2)}) collective-permute-start(bf16[2,4,128,256]{3,2,1,0:T(8,128)(2,1)S(1)} %pad_maximum_fusion.2), channel_id=1, source_target_pairs={{0,3},{1,2},{2,1},{3,0},{4,7},{5,6},{6,5},{7,4},{8,11},{9,10},{10,... | collective-permute-start | bytes 1572872 | tf_op jit(solution)/shard_map/ppermute | solution.py:59
  159.9 9.7 %collective-permute-done.28 = bf16[2,4,128,256]{3,2,1,0:T(8,128)(2,1)S(1)} collective-permute-done((bf16[2,4,128,256]{3,2,1,0:T(8,128)(2,1)S(1)}, bf16[2,4,128,256]{3,2,1,0:T(8,128)(2,1)S(1)}, u32[]{:S(2)}, u32[]{:S(2)}) %collective-permute-start.28) | collective-permute-done | bytes 524320 | tf_op jit(solution)/shard_map/ppermute | solution.py:59
  171.6 3.9 %collective-permute-start.27 = (bf16[2,4,128,256]{3,2,1,0:T(8,128)(2,1)S(1)}, bf16[2,4,128,256]{3,2,1,0:T(8,128)(2,1)S(1)}, u32[]{:S(2)}, u32[]{:S(2)}) collective-permute-start(bf16[2,4,128,256]{3,2,1,0:T(8,128)(2,1)S(1)} %pad_maximum_fusion.3), channel_id=1, source_target_pairs={{0,1},{1,0},{2,3},{3,2},{4,5},{5,4},{6,7},{7,6},{8,9},{9,8},{10,11... | collective-permute-start | bytes 1572872 | tf_op jit(solution)/shard_map/ppermute | solution.py:59
  177.5 9.0 %collective-permute-done.23.refs_10_ = bf16[4,128,256]{2,1,0:T(8,128)(2,1)S(1)} collective-permute-done((bf16[4,128,256]{2,1,0:T(8,128)(2,1)S(1)}, bf16[4,128,256]{2,1,0:T(8,128)(2,1)S(1)}, u32[]{:S(2)}, u32[]{:S(2)}) %collective-permute-start.23) | collective-permute-done | bytes 262176 | tf_op jit(solution)/shard_map/ppermute | solution.py:59
  188.4 3.9 %collective-permute-start.24 = (bf16[4,128,256]{2,1,0:T(8,128)(2,1)S(1)}, bf16[4,128,256]{2,1,0:T(8,128)(2,1)S(1)}, u32[]{:S(2)}, u32[]{:S(2)}) collective-permute-start(bf16[4,128,256]{2,1,0:T(8,128)(2,1)S(1)} %collective-permute-done.23.refs_10_), channel_id=1, source_target_pairs={{0,1},{1,0},{2,3},{3,2},{4,5},{5,4},{6,7},{7,6},{8,9},{9,8},{10,11... | collective-permute-start | bytes 786440 | tf_op jit(solution)/shard_map/ppermute | solution.py:59
  192.4 9.5 %collective-permute-done.24.refs_11_ = bf16[4,128,256]{2,1,0:T(8,128)(2,1)S(1)} collective-permute-done((bf16[4,128,256]{2,1,0:T(8,128)(2,1)S(1)}, bf16[4,128,256]{2,1,0:T(8,128)(2,1)S(1)}, u32[]{:S(2)}, u32[]{:S(2)}) %collective-permute-start.24) | collective-permute-done | bytes 262176 | tf_op jit(solution)/shard_map/ppermute | solution.py:59
  201.9 9.1 %shard_map.48 = (bf16[6,128,256]{2,1,0:T(8,128)(2,1)}, bf16[128,256]{1,0:T(8,128)(2,1)S(1)}, f32[128,256]{1,0:T(8,128)S(1)}) custom-call(s32[1,65]{1,0:T(1,128)S(1)} %copy-done.1, s32[1,128]{1,0:T(1,128)S(1)} %copy-done.2, s32[1]{0:T(128)} %bitcast.refs_2_, bf16[128,128,128]{2,1,0:T(8,128)(2,1)S(1)} %shard_map.46.refs_3_, bf16[8,128,256]{2,1,0:T(8,128)(2,1)S(1)} %bitcast.46, ...), custom_call_target="tpu_custom_call" | custom-call | tf_op jit(solution)/shard_map/pallas_call | solution.py:202
  213.2 6.1 %collective-permute-done.31 = bf16[128,256]{1,0:T(8,128)(2,1)S(1)} collective-permute-done((bf16[128,256]{1,0:T(8,128)(2,1)S(1)}, bf16[128,256]{1,0:T(8,128)(2,1)S(1)}, u32[]{:S(2)}, u32[]{:S(2)}) %collective-permute-start.31) | collective-permute-done | bytes 65568 | tf_op jit(solution)/shard_map/ppermute | solution.py:59
  (65 shorter events, 60.4 us)
Async XLA Ops:
  0.0 15.8 %collective-permute-start.4 = (bf16[4,128,256]{2,1,0:T(8,128)(2,1)}, bf16[4,128,256]{2,1,0:T(8,128)(2,1)S(1)}, u32[]{:S(2)}, u32[]{:S(2)}) collective-permute-start(bf16[4,128,256]{2,1,0:T(8,128)(2,1)} %bitcast.55), channel_id=1, source_target_pairs={{0,508},{1,509},{2,510},{3,511},{4,8},{5,9},{6,10},{7,11},{8,4},{9... | collective-permute-start | bytes 786440 | tf_op jit(solution)/shard_map/ppermute | solution.py:59
  2.0 15.7 %collective-permute-start = (bf16[4,128,256]{2,1,0:T(8,128)(2,1)}, bf16[4,128,256]{2,1,0:T(8,128)(2,1)S(1)}, u32[]{:S(2)}, u32[]{:S(2)}) collective-permute-start(bf16[4,128,256]{2,1,0:T(8,128)(2,1)} %bitcast.56), channel_id=1, source_target_pairs={{0,4},{1,5},{2,6},{3,7},{4,0},{5,1},{6,2},{7,3},{8,12},{9,13},{10,... | collective-permute-start | bytes 786440 | tf_op jit(solution)/shard_map/ppermute | solution.py:59
  17.7 15.9 %collective-permute-start.9 = (bf16[4,128,256]{2,1,0:T(8,128)(2,1)S(1)}, bf16[4,128,256]{2,1,0:T(8,128)(2,1)S(1)}, u32[]{:S(2)}, u32[]{:S(2)}) collective-permute-start(bf16[4,128,256]{2,1,0:T(8,128)(2,1)S(1)} %collective-permute-done), channel_id=1, source_target_pairs={{0,508},{1,509},{2,510},{3,511},{4,8},{5,9},{6,10},{7,11},{8,4},{9... | collective-permute-start | bytes 786440 | tf_op jit(solution)/shard_map/ppermute | solution.py:59
  33.7 23.5 %collective-permute-start.11 = (bf16[2,4,128,256]{3,2,1,0:T(8,128)(2,1)S(1)}, bf16[2,4,128,256]{3,2,1,0:T(8,128)(2,1)S(1)}, u32[]{:S(2)}, u32[]{:S(2)}) collective-permute-start(bf16[2,4,128,256]{3,2,1,0:T(8,128)(2,1)S(1)} %pad_maximum_fusion.1), channel_id=1, source_target_pairs={{0,3},{1,2},{2,1},{3,0},{4,7},{5,6},{6,5},{7,4},{8,11},{9,10},{10,... | collective-permute-start | bytes 1572872 | tf_op jit(solution)/shard_map/ppermute | solution.py:59
  39.6 23.5 %collective-permute-start.1 = (bf16[2,4,128,256]{3,2,1,0:T(8,128)(2,1)S(1)}, bf16[2,4,128,256]{3,2,1,0:T(8,128)(2,1)S(1)}, u32[]{:S(2)}, u32[]{:S(2)}) collective-permute-start(bf16[2,4,128,256]{3,2,1,0:T(8,128)(2,1)S(1)} %pad_maximum_fusion), channel_id=1, source_target_pairs={{0,1},{1,0},{2,3},{3,2},{4,5},{5,4},{6,7},{7,6},{8,9},{9,8},{10,11... | collective-permute-start | bytes 1572872 | tf_op jit(solution)/shard_map/ppermute | solution.py:59
  41.6 17.5 %collective-permute-start.12 = (bf16[4,128,256]{2,1,0:T(8,128)(2,1)}, bf16[4,128,256]{2,1,0:T(8,128)(2,1)S(1)}, u32[]{:S(2)}, u32[]{:S(2)}) collective-permute-start(bf16[4,128,256]{2,1,0:T(8,128)(2,1)} %bitcast.58), channel_id=1, source_target_pairs={{3,12},{7,16},{11,20},{15,24},{19,28},{23,32},{27,36},{31,40},{35,... | collective-permute-start | bytes 786440 | tf_op jit(solution)/shard_map/ppermute | solution.py:59
  43.6 46.5 %collective-permute-start.2 = (bf16[2,4,128,256]{3,2,1,0:T(8,128)(2,1)S(1)}, bf16[2,4,128,256]{3,2,1,0:T(8,128)(2,1)S(1)}, u32[]{:S(2)}, u32[]{:S(2)}) collective-permute-start(bf16[2,4,128,256]{3,2,1,0:T(8,128)(2,1)S(1)} %pad_maximum_fusion), channel_id=1, source_target_pairs={{0,3},{1,2},{2,1},{3,0},{4,7},{5,6},{6,5},{7,4},{8,11},{9,10},{10,... | collective-permute-start | bytes 1572872 | tf_op jit(solution)/shard_map/ppermute | solution.py:59
  46.6 27.4 %collective-permute-start.6 = (bf16[4,128,256]{2,1,0:T(8,128)(2,1)S(1)}, bf16[4,128,256]{2,1,0:T(8,128)(2,1)S(1)}, u32[]{:S(2)}, u32[]{:S(2)}) collective-permute-start(bf16[4,128,256]{2,1,0:T(8,128)(2,1)S(1)} %collective-permute-done.4.refs_8_), channel_id=1, source_target_pairs={{0,3},{1,2},{2,1},{3,0},{4,7},{5,6},{6,5},{7,4},{8,11},{9,10},{10,... | collective-permute-start | bytes 786440 | tf_op jit(solution)/shard_map/ppermute | solution.py:59
  57.1 18.8 %collective-permute-start.5 = (bf16[4,128,256]{2,1,0:T(8,128)(2,1)S(1)}, bf16[4,128,256]{2,1,0:T(8,128)(2,1)S(1)}, u32[]{:S(2)}, u32[]{:S(2)}) collective-permute-start(bf16[4,128,256]{2,1,0:T(8,128)(2,1)S(1)} %collective-permute-done.4.refs_8_), channel_id=1, source_target_pairs={{0,1},{1,0},{2,3},{3,2},{4,5},{5,4},{6,7},{7,6},{8,9},{9,8},{10,11... | collective-permute-start | bytes 786440 | tf_op jit(solution)/shard_map/ppermute | solution.py:59
  59.1 31.0 %collective-permute-start.10 = (bf16[2,4,128,256]{3,2,1,0:T(8,128)(2,1)S(1)}, bf16[2,4,128,256]{3,2,1,0:T(8,128)(2,1)S(1)}, u32[]{:S(2)}, u32[]{:S(2)}) collective-permute-start(bf16[2,4,128,256]{3,2,1,0:T(8,128)(2,1)S(1)} %pad_maximum_fusion.1), channel_id=1, source_target_pairs={{0,1},{1,0},{2,3},{3,2},{4,5},{5,4},{6,7},{7,6},{8,9},{9,8},{10,11... | collective-permute-start | bytes 1572872 | tf_op jit(solution)/shard_map/ppermute | solution.py:59
  63.1 27.1 %collective-permute-start.3 = (bf16[2,4,128,256]{3,2,1,0:T(8,128)(2,1)S(1)}, bf16[2,4,128,256]{3,2,1,0:T(8,128)(2,1)S(1)}, u32[]{:S(2)}, u32[]{:S(2)}) collective-permute-start(bf16[2,4,128,256]{3,2,1,0:T(8,128)(2,1)S(1)} %collective-permute-done.1), channel_id=1, source_target_pairs={{0,3},{1,2},{2,1},{3,0},{4,7},{5,6},{6,5},{7,4},{8,11},{9,10},{10,... | collective-permute-start | bytes 1572872 | tf_op jit(solution)/shard_map/ppermute | solution.py:59
  74.0 16.1 %collective-permute-start.13 = (bf16[5,128,256]{2,1,0:T(8,128)(2,1)S(1)}, bf16[5,128,256]{2,1,0:T(8,128)(2,1)S(1)}, u32[]{:S(2)}, u32[]{:S(2)}) collective-permute-start(bf16[5,128,256]{2,1,0:T(8,128)(2,1)S(1)} %pad_maximum_fusion.4), channel_id=1, source_target_pairs={{0,1},{1,0},{2,3},{3,2},{4,5},{5,4},{6,7},{7,6},{8,9},{9,8},{10,11... | collective-permute-start | bytes 983048 | tf_op jit(solution)/shard_map/ppermute | solution.py:59
  75.9 14.2 %collective-permute-start.7 = (bf16[4,128,256]{2,1,0:T(8,128)(2,1)S(1)}, bf16[4,128,256]{2,1,0:T(8,128)(2,1)S(1)}, u32[]{:S(2)}, u32[]{:S(2)}) collective-permute-start(bf16[4,128,256]{2,1,0:T(8,128)(2,1)S(1)} %collective-permute-done.6.refs_10_), channel_id=1, source_target_pairs={{0,1},{1,0},{2,3},{3,2},{4,5},{5,4},{6,7},{7,6},{8,9},{9,8},{10,11... | collective-permute-start | bytes 786440 | tf_op jit(solution)/shard_map/ppermute | solution.py:59
  115.1 15.7 %collective-permute-start.17 = (bf16[4,128,256]{2,1,0:T(8,128)(2,1)S(1)}, bf16[4,128,256]{2,1,0:T(8,128)(2,1)S(1)}, u32[]{:S(2)}, u32[]{:S(2)}) collective-permute-start(bf16[4,128,256]{2,1,0:T(8,128)(2,1)S(1)} %multiply_convert_fusion), channel_id=1, source_target_pairs={{0,4},{1,5},{2,6},{3,7},{4,0},{5,1},{6,2},{7,3},{8,12},{9,13},{10,... | collective-permute-start | bytes 786440 | tf_op jit(solution)/shard_map/ppermute | solution.py:59
  130.8 15.3 %collective-permute-start.26 = (bf16[4,128,256]{2,1,0:T(8,128)(2,1)S(1)}, bf16[4,128,256]{2,1,0:T(8,128)(2,1)S(1)}, u32[]{:S(2)}, u32[]{:S(2)}) collective-permute-start(bf16[4,128,256]{2,1,0:T(8,128)(2,1)S(1)} %collective-permute-done.17), channel_id=1, source_target_pairs={{0,508},{1,509},{2,510},{3,511},{4,8},{5,9},{6,10},{7,11},{8,4},{9... | collective-permute-start | bytes 786440 | tf_op jit(solution)/shard_map/ppermute | solution.py:59
  146.1 23.5 %collective-permute-start.28 = (bf16[2,4,128,256]{3,2,1,0:T(8,128)(2,1)S(1)}, bf16[2,4,128,256]{3,2,1,0:T(8,128)(2,1)S(1)}, u32[]{:S(2)}, u32[]{:S(2)}) collective-permute-start(bf16[2,4,128,256]{3,2,1,0:T(8,128)(2,1)S(1)} %pad_maximum_fusion.3), channel_id=1, source_target_pairs={{0,3},{1,2},{2,1},{3,0},{4,7},{5,6},{6,5},{7,4},{8,11},{9,10},{10,... | collective-permute-start | bytes 1572872 | tf_op jit(solution)/shard_map/ppermute | solution.py:59
  148.1 27.4 %collective-permute-start.18 = (bf16[2,4,128,256]{3,2,1,0:T(8,128)(2,1)S(1)}, bf16[2,4,128,256]{3,2,1,0:T(8,128)(2,1)S(1)}, u32[]{:S(2)}, u32[]{:S(2)}) collective-permute-start(bf16[2,4,128,256]{3,2,1,0:T(8,128)(2,1)S(1)} %pad_maximum_fusion.2), channel_id=1, source_target_pairs={{0,1},{1,0},{2,3},{3,2},{4,5},{5,4},{6,7},{7,6},{8,9},{9,8},{10,11... | collective-permute-start | bytes 1572872 | tf_op jit(solution)/shard_map/ppermute | solution.py:59
  150.8 20.8 %collective-permute-start.29 = (bf16[4,128,256]{2,1,0:T(8,128)(2,1)S(1)}, bf16[4,128,256]{2,1,0:T(8,128)(2,1)S(1)}, u32[]{:S(2)}, u32[]{:S(2)}) collective-permute-start(bf16[4,128,256]{2,1,0:T(8,128)(2,1)S(1)} %multiply_convert_fusion), channel_id=1, source_target_pairs={{3,12},{7,16},{11,20},{15,24},{19,28},{23,32},{27,36},{31,40},{35,... | collective-permute-start | bytes 786440 | tf_op jit(solution)/shard_map/ppermute | solution.py:59
  152.8 49.0 %collective-permute-start.19 = (bf16[2,4,128,256]{3,2,1,0:T(8,128)(2,1)S(1)}, bf16[2,4,128,256]{3,2,1,0:T(8,128)(2,1)S(1)}, u32[]{:S(2)}, u32[]{:S(2)}) collective-permute-start(bf16[2,4,128,256]{3,2,1,0:T(8,128)(2,1)S(1)} %pad_maximum_fusion.2), channel_id=1, source_target_pairs={{0,3},{1,2},{2,1},{3,0},{4,7},{5,6},{6,5},{7,4},{8,11},{9,10},{10,... | collective-permute-start | bytes 1572872 | tf_op jit(solution)/shard_map/ppermute | solution.py:59
  157.3 29.2 %collective-permute-start.23 = (bf16[4,128,256]{2,1,0:T(8,128)(2,1)S(1)}, bf16[4,128,256]{2,1,0:T(8,128)(2,1)S(1)}, u32[]{:S(2)}, u32[]{:S(2)}) collective-permute-start(bf16[4,128,256]{2,1,0:T(8,128)(2,1)S(1)} %collective-permute-done.21.refs_8_), channel_id=1, source_target_pairs={{0,3},{1,2},{2,1},{3,0},{4,7},{5,6},{6,5},{7,4},{8,11},{9,10},{10,... | collective-permute-start | bytes 786440 | tf_op jit(solution)/shard_map/ppermute | solution.py:59
  169.6 18.8 %collective-permute-start.22 = (bf16[4,128,256]{2,1,0:T(8,128)(2,1)S(1)}, bf16[4,128,256]{2,1,0:T(8,128)(2,1)S(1)}, u32[]{:S(2)}, u32[]{:S(2)}) collective-permute-start(bf16[4,128,256]{2,1,0:T(8,128)(2,1)S(1)} %collective-permute-done.21.refs_8_), channel_id=1, source_target_pairs={{0,1},{1,0},{2,3},{3,2},{4,5},{5,4},{6,7},{7,6},{8,9},{9,8},{10,11... | collective-permute-start | bytes 786440 | tf_op jit(solution)/shard_map/ppermute | solution.py:59
  171.6 30.2 %collective-permute-start.27 = (bf16[2,4,128,256]{3,2,1,0:T(8,128)(2,1)S(1)}, bf16[2,4,128,256]{3,2,1,0:T(8,128)(2,1)S(1)}, u32[]{:S(2)}, u32[]{:S(2)}) collective-permute-start(bf16[2,4,128,256]{3,2,1,0:T(8,128)(2,1)S(1)} %pad_maximum_fusion.3), channel_id=1, source_target_pairs={{0,1},{1,0},{2,3},{3,2},{4,5},{5,4},{6,7},{7,6},{8,9},{9,8},{10,11... | collective-permute-start | bytes 1572872 | tf_op jit(solution)/shard_map/ppermute | solution.py:59
  175.6 26.3 %collective-permute-start.20 = (bf16[2,4,128,256]{3,2,1,0:T(8,128)(2,1)S(1)}, bf16[2,4,128,256]{3,2,1,0:T(8,128)(2,1)S(1)}, u32[]{:S(2)}, u32[]{:S(2)}) collective-permute-start(bf16[2,4,128,256]{3,2,1,0:T(8,128)(2,1)S(1)} %collective-permute-done.18), channel_id=1, source_target_pairs={{0,3},{1,2},{2,1},{3,0},{4,7},{5,6},{6,5},{7,4},{8,11},{9,10},{10,... | collective-permute-start | bytes 1572872 | tf_op jit(solution)/shard_map/ppermute | solution.py:59
  186.5 15.4 %collective-permute-start.30 = (bf16[5,128,256]{2,1,0:T(8,128)(2,1)S(1)}, bf16[5,128,256]{2,1,0:T(8,128)(2,1)S(1)}, u32[]{:S(2)}, u32[]{:S(2)}) collective-permute-start(bf16[5,128,256]{2,1,0:T(8,128)(2,1)S(1)} %pad_maximum_fusion.5), channel_id=1, source_target_pairs={{0,1},{1,0},{2,3},{3,2},{4,5},{5,4},{6,7},{7,6},{8,9},{9,8},{10,11... | collective-permute-start | bytes 983048 | tf_op jit(solution)/shard_map/ppermute | solution.py:59
  (12 other events, 162.0 us)
where the time goes:
time: 221 us; the launch traced here: 220 us
  waiting for transfers between devices  101 us (46%)
  starting transfers between devices  96.6 us (44%)
  Pallas kernels  17.8 us (8%)
    ppermute x32, waiting for transfers between devices, send(): return lax.ppermute(value, AXES, pairs)  101 us
    ppermute x32, starting transfers between devices, send(): return lax.ppermute(value, AXES, pairs)  96.6 us
    pallas_call x2, Pallas kernels, call_products(): pl.pallas_call(kernel, out_shape=outs, in_specs=[smem] * 3 + [vmem] + [hb...  17.5 us
  transfers between devices with their start and end apart: 32, of which 14 were waited for; matrix products, arithmetic and copies ran while one was open for 1% of the time, Pallas kernels for 0%

commit v1 on v0

--- a/solution.py
+++ b/solution.py
@@ -12,7 +12,7 @@
 HOME = 4
 NNZ = 128
 ROWS = 64
-DEPTH = 4
+DEPTH = 16
 HALF = 32
 WIN = ROWS + 2 * HALF
 DEVICES = 512
@@ -38,6 +38,10 @@
 
 def shift_dev(step):
     return [(g, g + step) for g in range(DEVICES) if 0 <= g % 16 + step < 16]
+
+
+def cross_y():
+    return [(g, g ^ 2) for g in range(DEVICES)]
 
 
 def swap_dev(odd):
@@ -70,17 +74,17 @@
     far_a = send(next_b, swap_z(0))
     first_a = send(first, swap_y(0))
     first_b = send(first, swap_y(1))
-    first_x = send(first_a, swap_y(1))
+    first_x = send(first, cross_y())
     second_a = send(next_b, swap_y(0))
     second_b = send(next_b, swap_y(1))
-    second_x = send(second_b, swap_y(0))
+    second_x = send(jnp.concatenate([second_b, edge[:1]]), swap_y(0))
     third = jnp.stack([far_a, far_b])
     third_a = send(third, swap_y(0))
     third_b = send(third, swap_y(1))
-    wants_far_b = lower == (side == 1)
-    wanted = jnp.where(wants_far_b, third_b[1], third_b[0])
-    other = jnp.where(wants_far_b, third_b[0, :1], third_b[1, :1])
-    last = send(jnp.concatenate([wanted, jnp.where(lower, other, edge[:1])]), swap_y(0))
+    sends_far_b = lower == (side == 1)
+    wanted = jnp.where(sends_far_b, far_a, far_b)
+    other = jnp.where(sends_far_b, far_b, far_a)
+    last = send(jnp.concatenate([wanted, other[:1]]), cross_y())
     arrays = [first, first_a, first_b, first_x]
     arrays += [next_b, second_a, second_b, second_x, third, third_a, third_b, last, edge]
     arrays = [array.reshape(-1, BLK, VEC) for array in arrays]
@@ -106,8 +110,10 @@
         pieces += [(8 + array, 4 * i, HOME, at(offset, source)) for i, offset in enumerate(offsets)]
     lower = y < 2
     pieces.append((11, 0, HOME, at(jnp.where(lower, -2, 2), y ^ 2)))
-    single = jnp.where(lower, at(2, y ^ 2), at(3, y - 2))
-    pieces.append((11, HOME, 1, jnp.where(single < WIN, single, -1)))
+    pieces.append((11, HOME, 1, jnp.where(lower, at(2, y ^ 2), -1)))
+    next_up = at(3, y - 2)
+    reaches = jnp.logical_and(y >= 2, next_up < WIN)
+    pieces.append((7, HOME, 1, jnp.where(reaches, next_up, -1)))
     whole = jnp.where(y == 0, at(-3, 3), jnp.where(y == 3, at(3, 0), -1))
     pieces.append((12, 0, HOME, jnp.where(whole < WIN, whole, -1)))
     return pieces

time: 221 us -> 222 us (level)
  the two profiles are of different devices: /device:TPU:70 before, /device:TPU:230 now
where the time goes in v1:
time: 222 us; the launch traced here: 221 us
  starting transfers between devices  115 us (52%)
  waiting for transfers between devices  91.3 us (41%)
  Pallas kernels  11.5 us (5%)
  other arithmetic  2.4 us (1%)
    ppermute x32, starting transfers between devices, send(): return lax.ppermute(value, AXES, pairs)  115 us
    ppermute x32, waiting for transfers between devices, send(): return lax.ppermute(value, AXES, pairs)  91.3 us
    pallas_call x2, Pallas kernels, call_products(): pl.pallas_call(kernel, out_shape=outs, in_specs=[smem] * 3 + [vmem] + [hb...  11.2 us
  transfers between devices with their start and end apart: 32, of which 11 were waited for; matrix products, arithmetic and copies ran while one was open for 1% of the time, Pallas kernels for 0%

profile of v1, /device:TPU:230, one launch (start us, length us, event | category | flops | bytes accessed | tf_op | source)
XLA Modules:
  0.0 221.2 jit_solution(9754958268530295520)
XLA Ops:
  4.0 7.7 %collective-permute-start.7 = (bf16[4,128,256]{2,1,0:T(8,128)(2,1)}, bf16[4,128,256]{2,1,0:T(8,128)(2,1)S(1)}, u32[]{:S(2)}, u32[]{:S(2)}) collective-permute-start(bf16[4,128,256]{2,1,0:T(8,128)(2,1)} %bitcast.49), channel_id=1, source_target_pairs={{3,12},{7,16},{11,20},{15,24},{19,28},{23,32},{27,36},{31,40},{35,... | collective-permute-start | bytes 786440 | tf_op jit(solution)/shard_map/ppermute | solution.py:63
  12.4 6.5 %collective-permute-start.9 = (bf16[4,128,256]{2,1,0:T(8,128)(2,1)S(1)}, bf16[4,128,256]{2,1,0:T(8,128)(2,1)S(1)}, u32[]{:S(2)}, u32[]{:S(2)}) collective-permute-start(bf16[4,128,256]{2,1,0:T(8,128)(2,1)S(1)} %collective-permute-done.4.refs_8_), channel_id=1, source_target_pairs={{0,4},{1,5},{2,6},{3,7},{4,0},{5,1},{6,2},{7,3},{8,12},{9,13},{10,... | collective-permute-start | bytes 786440 | tf_op jit(solution)/shard_map/ppermute | solution.py:63
  22.0 4.4 %collective-permute-start.3 = (bf16[2,4,128,256]{3,2,1,0:T(8,128)(2,1)S(1)}, bf16[2,4,128,256]{3,2,1,0:T(8,128)(2,1)S(1)}, u32[]{:S(2)}, u32[]{:S(2)}) collective-permute-start(bf16[2,4,128,256]{3,2,1,0:T(8,128)(2,1)S(1)} %pad_maximum_fusion), channel_id=1, source_target_pairs={{0,2},{1,3},{2,0},{3,1},{4,6},{5,7},{6,4},{7,5},{8,10},{9,11},{10,... | collective-permute-start | bytes 1572872 | tf_op jit(solution)/shard_map/ppermute | solution.py:63
  26.5 5.4 %collective-permute-start.2 = (bf16[2,4,128,256]{3,2,1,0:T(8,128)(2,1)S(1)}, bf16[2,4,128,256]{3,2,1,0:T(8,128)(2,1)S(1)}, u32[]{:S(2)}, u32[]{:S(2)}) collective-permute-start(bf16[2,4,128,256]{3,2,1,0:T(8,128)(2,1)S(1)} %pad_maximum_fusion), channel_id=1, source_target_pairs={{0,3},{1,2},{2,1},{3,0},{4,7},{5,6},{6,5},{7,4},{8,11},{9,10},{10,... | collective-permute-start | bytes 1572872 | tf_op jit(solution)/shard_map/ppermute | solution.py:63
  34.7 4.5 %collective-permute-start.6 = (bf16[4,128,256]{2,1,0:T(8,128)(2,1)S(1)}, bf16[4,128,256]{2,1,0:T(8,128)(2,1)S(1)}, u32[]{:S(2)}, u32[]{:S(2)}) collective-permute-start(bf16[4,128,256]{2,1,0:T(8,128)(2,1)S(1)} %collective-permute-done.4.refs_8_), channel_id=1, source_target_pairs={{0,3},{1,2},{2,1},{3,0},{4,7},{5,6},{6,5},{7,4},{8,11},{9,10},{10,... | collective-permute-start | bytes 786440 | tf_op jit(solution)/shard_map/ppermute | solution.py:63
  41.2 18.2 %collective-permute-done.6.refs_10_ = bf16[4,128,256]{2,1,0:T(8,128)(2,1)S(1)} collective-permute-done((bf16[4,128,256]{2,1,0:T(8,128)(2,1)S(1)}, bf16[4,128,256]{2,1,0:T(8,128)(2,1)S(1)}, u32[]{:S(2)}, u32[]{:S(2)}) %collective-permute-start.6) | collective-permute-done | bytes 262176 | tf_op jit(solution)/shard_map/ppermute | solution.py:63
  59.5 5.6 %collective-permute-start.12 = (bf16[2,4,128,256]{3,2,1,0:T(8,128)(2,1)S(1)}, bf16[2,4,128,256]{3,2,1,0:T(8,128)(2,1)S(1)}, u32[]{:S(2)}, u32[]{:S(2)}) collective-permute-start(bf16[2,4,128,256]{3,2,1,0:T(8,128)(2,1)S(1)} %pad_maximum_fusion.1), channel_id=1, source_target_pairs={{0,3},{1,2},{2,1},{3,0},{4,7},{5,6},{6,5},{7,4},{8,11},{9,10},{10,... | collective-permute-start | bytes 1572872 | tf_op jit(solution)/shard_map/ppermute | solution.py:63
  67.1 3.4 %collective-permute-start.13 = (bf16[5,128,256]{2,1,0:T(8,128)(2,1)S(1)}, bf16[5,128,256]{2,1,0:T(8,128)(2,1)S(1)}, u32[]{:S(2)}, u32[]{:S(2)}) collective-permute-start(bf16[5,128,256]{2,1,0:T(8,128)(2,1)S(1)} %pad_maximum_fusion.5), channel_id=1, source_target_pairs={{0,2},{1,3},{2,0},{3,1},{4,6},{5,7},{6,4},{7,5},{8,10},{9,11},{10,... | collective-permute-start | bytes 983048 | tf_op jit(solution)/shard_map/ppermute | solution.py:63
  73.3 14.9 %collective-permute-done.13.refs_15_ = bf16[5,128,256]{2,1,0:T(8,128)(2,1)S(1)} collective-permute-done((bf16[5,128,256]{2,1,0:T(8,128)(2,1)S(1)}, bf16[5,128,256]{2,1,0:T(8,128)(2,1)S(1)}, u32[]{:S(2)}, u32[]{:S(2)}) %collective-permute-start.13) | collective-permute-done | bytes 327712 | tf_op jit(solution)/shard_map/ppermute | solution.py:63
  88.3 6.4 %collective-permute-done.8.refs_11_ = bf16[5,128,256]{2,1,0:T(8,128)(2,1)S(1)} collective-permute-done((bf16[5,128,256]{2,1,0:T(8,128)(2,1)S(1)}, bf16[5,128,256]{2,1,0:T(8,128)(2,1)S(1)}, u32[]{:S(2)}, u32[]{:S(2)}) %collective-permute-start.8) | collective-permute-done | bytes 327712 | tf_op jit(solution)/shard_map/ppermute | solution.py:63
  94.7 5.2 %shard_map.47 = (bf16[4,128,256]{2,1,0:T(8,128)(2,1)S(1)}, f32[4,128,256]{2,1,0:T(8,128)S(1)}, bf16[4,128,256]{2,1,0:T(8,128)(2,1)S(1)}, bf16[1,128,256]{2,1,0:T(8,128)(2,1)S(1)}, bf16[6,128,256]{2,1,0:T(8,128)(2,1)S(1)}) custom-call(s32[1,65]{1,0:T(1,128)S(1)} %copy-done.1, s32[1,128]{1,0:T(1,128)S(1)} %copy-done.2, s32[1]{0:T(128)} %bitcast.refs_2_, ...), custom_call_target="tpu_custom_call" | custom-call | tf_op jit(solution)/shard_map/pallas_call | solution.py:208
  104.9 4.8 %collective-permute-start.16 = (bf16[1,128,256]{2,1,0:T(8,128)(2,1)S(1)}, bf16[1,128,256]{2,1,0:T(8,128)(2,1)S(1)}, u32[]{:S(2)}, u32[]{:S(2)}) collective-permute-start(bf16[1,128,256]{2,1,0:T(8,128)(2,1)S(1)} %get-tuple-element.42), channel_id=1, source_target_pairs={{0,2},{1,3},{2,4},{3,5},{4,6},{5,7},{6,8},{7,9},{8,10},{9,11},{10,... | collective-permute-start | bytes 196616 | tf_op jit(solution)/shard_map/ppermute | solution.py:63
  109.8 5.1 %collective-permute-done.15 = bf16[4,128,256]{2,1,0:T(8,128)(2,1)S(1)} collective-permute-done((bf16[4,128,256]{2,1,0:T(8,128)(2,1)S(1)}, bf16[4,128,256]{2,1,0:T(8,128)(2,1)S(1)}, u32[]{:S(2)}, u32[]{:S(2)}) %collective-permute-start.15) | collective-permute-done | bytes 262176 | tf_op jit(solution)/shard_map/ppermute | solution.py:63
  119.5 5.1 %collective-permute-start.24 = (bf16[4,128,256]{2,1,0:T(8,128)(2,1)S(1)}, bf16[4,128,256]{2,1,0:T(8,128)(2,1)S(1)}, u32[]{:S(2)}, u32[]{:S(2)}) collective-permute-start(bf16[4,128,256]{2,1,0:T(8,128)(2,1)S(1)} %multiply_convert_fusion), channel_id=1, source_target_pairs={{3,12},{7,16},{11,20},{15,24},{19,28},{23,32},{27,36},{31,40},{35,... | collective-permute-start | bytes 786440 | tf_op jit(solution)/shard_map/ppermute | solution.py:63
  125.5 6.0 %collective-permute-start.26 = (bf16[4,128,256]{2,1,0:T(8,128)(2,1)S(1)}, bf16[4,128,256]{2,1,0:T(8,128)(2,1)S(1)}, u32[]{:S(2)}, u32[]{:S(2)}) collective-permute-start(bf16[4,128,256]{2,1,0:T(8,128)(2,1)S(1)} %collective-permute-done.21.refs_8_), channel_id=1, source_target_pairs={{0,4},{1,5},{2,6},{3,7},{4,0},{5,1},{6,2},{7,3},{8,12},{9,13},{10,... | collective-permute-start | bytes 786440 | tf_op jit(solution)/shard_map/ppermute | solution.py:63
  131.5 8.2 %collective-permute-start.27 = (bf16[4,128,256]{2,1,0:T(8,128)(2,1)S(1)}, bf16[4,128,256]{2,1,0:T(8,128)(2,1)S(1)}, u32[]{:S(2)}, u32[]{:S(2)}) collective-permute-start(bf16[4,128,256]{2,1,0:T(8,128)(2,1)S(1)} %collective-permute-done.17), channel_id=1, source_target_pairs={{0,508},{1,509},{2,510},{3,511},{4,8},{5,9},{6,10},{7,11},{8,4},{9... | collective-permute-start | bytes 786440 | tf_op jit(solution)/shard_map/ppermute | solution.py:63
  141.6 5.8 %collective-permute-start.19 = (bf16[2,4,128,256]{3,2,1,0:T(8,128)(2,1)S(1)}, bf16[2,4,128,256]{3,2,1,0:T(8,128)(2,1)S(1)}, u32[]{:S(2)}, u32[]{:S(2)}) collective-permute-start(bf16[2,4,128,256]{3,2,1,0:T(8,128)(2,1)S(1)} %pad_maximum_fusion.2), channel_id=1, source_target_pairs={{0,3},{1,2},{2,1},{3,0},{4,7},{5,6},{6,5},{7,4},{8,11},{9,10},{10,... | collective-permute-start | bytes 1572872 | tf_op jit(solution)/shard_map/ppermute | solution.py:63
  151.5 3.8 %collective-permute-start.22 = (bf16[4,128,256]{2,1,0:T(8,128)(2,1)S(1)}, bf16[4,128,256]{2,1,0:T(8,128)(2,1)S(1)}, u32[]{:S(2)}, u32[]{:S(2)}) collective-permute-start(bf16[4,128,256]{2,1,0:T(8,128)(2,1)S(1)} %collective-permute-done.21.refs_8_), channel_id=1, source_target_pairs={{0,1},{1,0},{2,3},{3,2},{4,5},{5,4},{6,7},{7,6},{8,9},{9,8},{10,11... | collective-permute-start | bytes 786440 | tf_op jit(solution)/shard_map/ppermute | solution.py:63
  155.4 19.1 %collective-permute-done.23.refs_10_ = bf16[4,128,256]{2,1,0:T(8,128)(2,1)S(1)} collective-permute-done((bf16[4,128,256]{2,1,0:T(8,128)(2,1)S(1)}, bf16[4,128,256]{2,1,0:T(8,128)(2,1)S(1)}, u32[]{:S(2)}, u32[]{:S(2)}) %collective-permute-start.23) | collective-permute-done | bytes 262176 | tf_op jit(solution)/shard_map/ppermute | solution.py:63
  178.6 6.4 %collective-permute-start.30 = (bf16[5,128,256]{2,1,0:T(8,128)(2,1)S(1)}, bf16[5,128,256]{2,1,0:T(8,128)(2,1)S(1)}, u32[]{:S(2)}, u32[]{:S(2)}) collective-permute-start(bf16[5,128,256]{2,1,0:T(8,128)(2,1)S(1)} %pad_maximum_fusion.7), channel_id=1, source_target_pairs={{0,2},{1,3},{2,0},{3,1},{4,6},{5,7},{6,4},{7,5},{8,10},{9,11},{10,... | collective-permute-start | bytes 983048 | tf_op jit(solution)/shard_map/ppermute | solution.py:63
  187.0 15.8 %collective-permute-done.30.refs_15_ = bf16[5,128,256]{2,1,0:T(8,128)(2,1)S(1)} collective-permute-done((bf16[5,128,256]{2,1,0:T(8,128)(2,1)S(1)}, bf16[5,128,256]{2,1,0:T(8,128)(2,1)S(1)}, u32[]{:S(2)}, u32[]{:S(2)}) %collective-permute-start.30) | collective-permute-done | bytes 327712 | tf_op jit(solution)/shard_map/ppermute | solution.py:63
  202.8 3.4 %collective-permute-done.25.refs_11_ = bf16[5,128,256]{2,1,0:T(8,128)(2,1)S(1)} collective-permute-done((bf16[5,128,256]{2,1,0:T(8,128)(2,1)S(1)}, bf16[5,128,256]{2,1,0:T(8,128)(2,1)S(1)}, u32[]{:S(2)}, u32[]{:S(2)}) %collective-permute-start.25) | collective-permute-done | bytes 327712 | tf_op jit(solution)/shard_map/ppermute | solution.py:63
  206.3 6.0 %shard_map.48 = (bf16[6,128,256]{2,1,0:T(8,128)(2,1)}, bf16[128,256]{1,0:T(8,128)(2,1)S(1)}, f32[128,256]{1,0:T(8,128)S(1)}) custom-call(s32[1,65]{1,0:T(1,128)S(1)} %copy-done.1, s32[1,128]{1,0:T(1,128)S(1)} %copy-done.2, s32[1]{0:T(128)} %bitcast.refs_2_, bf16[128,128,128]{2,1,0:T(8,128)(2,1)S(1)} %shard_map.46.refs_3_, bf16[8,128,256]{2,1,0:T(8,128)(2,1)S(1)} %bitcast.31, ...), custom_call_target="tpu_custom_call" | custom-call | tf_op jit(solution)/shard_map/pallas_call | solution.py:208
  214.4 6.1 %collective-permute-done.31 = bf16[128,256]{1,0:T(8,128)(2,1)S(1)} collective-permute-done((bf16[128,256]{1,0:T(8,128)(2,1)S(1)}, bf16[128,256]{1,0:T(8,128)(2,1)S(1)}, u32[]{:S(2)}, u32[]{:S(2)}) %collective-permute-start.31) | collective-permute-done | bytes 65568 | tf_op jit(solution)/shard_map/ppermute | solution.py:63
  (69 shorter events, 42.6 us)
Async XLA Ops:
  4.0 28.4 %collective-permute-start.7 = (bf16[4,128,256]{2,1,0:T(8,128)(2,1)}, bf16[4,128,256]{2,1,0:T(8,128)(2,1)S(1)}, u32[]{:S(2)}, u32[]{:S(2)}) collective-permute-start(bf16[4,128,256]{2,1,0:T(8,128)(2,1)} %bitcast.49), channel_id=1, source_target_pairs={{3,12},{7,16},{11,20},{15,24},{19,28},{23,32},{27,36},{31,40},{35,... | collective-permute-start | bytes 786440 | tf_op jit(solution)/shard_map/ppermute | solution.py:63
  12.4 22.2 %collective-permute-start.9 = (bf16[4,128,256]{2,1,0:T(8,128)(2,1)S(1)}, bf16[4,128,256]{2,1,0:T(8,128)(2,1)S(1)}, u32[]{:S(2)}, u32[]{:S(2)}) collective-permute-start(bf16[4,128,256]{2,1,0:T(8,128)(2,1)S(1)} %collective-permute-done.4.refs_8_), channel_id=1, source_target_pairs={{0,4},{1,5},{2,6},{3,7},{4,0},{5,1},{6,2},{7,3},{8,12},{9,13},{10,... | collective-permute-start | bytes 786440 | tf_op jit(solution)/shard_map/ppermute | solution.py:63
  18.9 20.3 %collective-permute-start.10 = (bf16[4,128,256]{2,1,0:T(8,128)(2,1)S(1)}, bf16[4,128,256]{2,1,0:T(8,128)(2,1)S(1)}, u32[]{:S(2)}, u32[]{:S(2)}) collective-permute-start(bf16[4,128,256]{2,1,0:T(8,128)(2,1)S(1)} %collective-permute-done), channel_id=1, source_target_pairs={{0,508},{1,509},{2,510},{3,511},{4,8},{5,9},{6,10},{7,11},{8,4},{9... | collective-permute-start | bytes 786440 | tf_op jit(solution)/shard_map/ppermute | solution.py:63
  22.0 45.1 %collective-permute-start.3 = (bf16[2,4,128,256]{3,2,1,0:T(8,128)(2,1)S(1)}, bf16[2,4,128,256]{3,2,1,0:T(8,128)(2,1)S(1)}, u32[]{:S(2)}, u32[]{:S(2)}) collective-permute-start(bf16[2,4,128,256]{3,2,1,0:T(8,128)(2,1)S(1)} %pad_maximum_fusion), channel_id=1, source_target_pairs={{0,2},{1,3},{2,0},{3,1},{4,6},{5,7},{6,4},{7,5},{8,10},{9,11},{10,... | collective-permute-start | bytes 1572872 | tf_op jit(solution)/shard_map/ppermute | solution.py:63
  26.5 44.0 %collective-permute-start.2 = (bf16[2,4,128,256]{3,2,1,0:T(8,128)(2,1)S(1)}, bf16[2,4,128,256]{3,2,1,0:T(8,128)(2,1)S(1)}, u32[]{:S(2)}, u32[]{:S(2)}) collective-permute-start(bf16[2,4,128,256]{3,2,1,0:T(8,128)(2,1)S(1)} %pad_maximum_fusion), channel_id=1, source_target_pairs={{0,3},{1,2},{2,1},{3,0},{4,7},{5,6},{6,5},{7,4},{8,11},{9,10},{10,... | collective-permute-start | bytes 1572872 | tf_op jit(solution)/shard_map/ppermute | solution.py:63
  32.4 40.9 %collective-permute-start.1 = (bf16[2,4,128,256]{3,2,1,0:T(8,128)(2,1)S(1)}, bf16[2,4,128,256]{3,2,1,0:T(8,128)(2,1)S(1)}, u32[]{:S(2)}, u32[]{:S(2)}) collective-permute-start(bf16[2,4,128,256]{3,2,1,0:T(8,128)(2,1)S(1)} %pad_maximum_fusion), channel_id=1, source_target_pairs={{0,1},{1,0},{2,3},{3,2},{4,5},{5,4},{6,7},{7,6},{8,9},{9,8},{10,11... | collective-permute-start | bytes 1572872 | tf_op jit(solution)/shard_map/ppermute | solution.py:63
  34.7 24.8 %collective-permute-start.6 = (bf16[4,128,256]{2,1,0:T(8,128)(2,1)S(1)}, bf16[4,128,256]{2,1,0:T(8,128)(2,1)S(1)}, u32[]{:S(2)}, u32[]{:S(2)}) collective-permute-start(bf16[4,128,256]{2,1,0:T(8,128)(2,1)S(1)} %collective-permute-done.4.refs_8_), channel_id=1, source_target_pairs={{0,3},{1,2},{2,1},{3,0},{4,7},{5,6},{6,5},{7,4},{8,11},{9,10},{10,... | collective-permute-start | bytes 786440 | tf_op jit(solution)/shard_map/ppermute | solution.py:63
  39.2 25.9 %collective-permute-start.5 = (bf16[4,128,256]{2,1,0:T(8,128)(2,1)S(1)}, bf16[4,128,256]{2,1,0:T(8,128)(2,1)S(1)}, u32[]{:S(2)}, u32[]{:S(2)}) collective-permute-start(bf16[4,128,256]{2,1,0:T(8,128)(2,1)S(1)} %collective-permute-done.4.refs_8_), channel_id=1, source_target_pairs={{0,1},{1,0},{2,3},{3,2},{4,5},{5,4},{6,7},{7,6},{8,9},{9,8},{10,11... | collective-permute-start | bytes 786440 | tf_op jit(solution)/shard_map/ppermute | solution.py:63
  59.5 35.2 %collective-permute-start.12 = (bf16[2,4,128,256]{3,2,1,0:T(8,128)(2,1)S(1)}, bf16[2,4,128,256]{3,2,1,0:T(8,128)(2,1)S(1)}, u32[]{:S(2)}, u32[]{:S(2)}) collective-permute-start(bf16[2,4,128,256]{3,2,1,0:T(8,128)(2,1)S(1)} %pad_maximum_fusion.1), channel_id=1, source_target_pairs={{0,3},{1,2},{2,1},{3,0},{4,7},{5,6},{6,5},{7,4},{8,11},{9,10},{10,... | collective-permute-start | bytes 1572872 | tf_op jit(solution)/shard_map/ppermute | solution.py:63
  65.1 29.6 %collective-permute-start.11 = (bf16[2,4,128,256]{3,2,1,0:T(8,128)(2,1)S(1)}, bf16[2,4,128,256]{3,2,1,0:T(8,128)(2,1)S(1)}, u32[]{:S(2)}, u32[]{:S(2)}) collective-permute-start(bf16[2,4,128,256]{3,2,1,0:T(8,128)(2,1)S(1)} %pad_maximum_fusion.1), channel_id=1, source_target_pairs={{0,1},{1,0},{2,3},{3,2},{4,5},{5,4},{6,7},{7,6},{8,9},{9,8},{10,11... | collective-permute-start | bytes 1572872 | tf_op jit(solution)/shard_map/ppermute | solution.py:63
  67.1 21.1 %collective-permute-start.13 = (bf16[5,128,256]{2,1,0:T(8,128)(2,1)S(1)}, bf16[5,128,256]{2,1,0:T(8,128)(2,1)S(1)}, u32[]{:S(2)}, u32[]{:S(2)}) collective-permute-start(bf16[5,128,256]{2,1,0:T(8,128)(2,1)S(1)} %pad_maximum_fusion.5), channel_id=1, source_target_pairs={{0,2},{1,3},{2,0},{3,1},{4,6},{5,7},{6,4},{7,5},{8,10},{9,11},{10,... | collective-permute-start | bytes 983048 | tf_op jit(solution)/shard_map/ppermute | solution.py:63
  70.5 24.2 %collective-permute-start.8 = (bf16[5,128,256]{2,1,0:T(8,128)(2,1)S(1)}, bf16[5,128,256]{2,1,0:T(8,128)(2,1)S(1)}, u32[]{:S(2)}, u32[]{:S(2)}) collective-permute-start(bf16[5,128,256]{2,1,0:T(8,128)(2,1)S(1)} %pad_maximum_fusion.4), channel_id=1, source_target_pairs={{0,1},{1,0},{2,3},{3,2},{4,5},{5,4},{6,7},{7,6},{8,9},{9,8},{10,11... | collective-permute-start | bytes 983048 | tf_op jit(solution)/shard_map/ppermute | solution.py:63
  119.5 28.0 %collective-permute-start.24 = (bf16[4,128,256]{2,1,0:T(8,128)(2,1)S(1)}, bf16[4,128,256]{2,1,0:T(8,128)(2,1)S(1)}, u32[]{:S(2)}, u32[]{:S(2)}) collective-permute-start(bf16[4,128,256]{2,1,0:T(8,128)(2,1)S(1)} %multiply_convert_fusion), channel_id=1, source_target_pairs={{3,12},{7,16},{11,20},{15,24},{19,28},{23,32},{27,36},{31,40},{35,... | collective-permute-start | bytes 786440 | tf_op jit(solution)/shard_map/ppermute | solution.py:63
  125.5 24.0 %collective-permute-start.26 = (bf16[4,128,256]{2,1,0:T(8,128)(2,1)S(1)}, bf16[4,128,256]{2,1,0:T(8,128)(2,1)S(1)}, u32[]{:S(2)}, u32[]{:S(2)}) collective-permute-start(bf16[4,128,256]{2,1,0:T(8,128)(2,1)S(1)} %collective-permute-done.21.refs_8_), channel_id=1, source_target_pairs={{0,4},{1,5},{2,6},{3,7},{4,0},{5,1},{6,2},{7,3},{8,12},{9,13},{10,... | collective-permute-start | bytes 786440 | tf_op jit(solution)/shard_map/ppermute | solution.py:63
  131.5 20.0 %collective-permute-start.27 = (bf16[4,128,256]{2,1,0:T(8,128)(2,1)S(1)}, bf16[4,128,256]{2,1,0:T(8,128)(2,1)S(1)}, u32[]{:S(2)}, u32[]{:S(2)}) collective-permute-start(bf16[4,128,256]{2,1,0:T(8,128)(2,1)S(1)} %collective-permute-done.17), channel_id=1, source_target_pairs={{0,508},{1,509},{2,510},{3,511},{4,8},{5,9},{6,10},{7,11},{8,4},{9... | collective-permute-start | bytes 786440 | tf_op jit(solution)/shard_map/ppermute | solution.py:63
  139.7 38.9 %collective-permute-start.20 = (bf16[2,4,128,256]{3,2,1,0:T(8,128)(2,1)S(1)}, bf16[2,4,128,256]{3,2,1,0:T(8,128)(2,1)S(1)}, u32[]{:S(2)}, u32[]{:S(2)}) collective-permute-start(bf16[2,4,128,256]{3,2,1,0:T(8,128)(2,1)S(1)} %pad_maximum_fusion.2), channel_id=1, source_target_pairs={{0,2},{1,3},{2,0},{3,1},{4,6},{5,7},{6,4},{7,5},{8,10},{9,11},{10,... | collective-permute-start | bytes 1572872 | tf_op jit(solution)/shard_map/ppermute | solution.py:63
  141.6 43.4 %collective-permute-start.19 = (bf16[2,4,128,256]{3,2,1,0:T(8,128)(2,1)S(1)}, bf16[2,4,128,256]{3,2,1,0:T(8,128)(2,1)S(1)}, u32[]{:S(2)}, u32[]{:S(2)}) collective-permute-start(bf16[2,4,128,256]{3,2,1,0:T(8,128)(2,1)S(1)} %pad_maximum_fusion.2), channel_id=1, source_target_pairs={{0,3},{1,2},{2,1},{3,0},{4,7},{5,6},{6,5},{7,4},{8,11},{9,10},{10,... | collective-permute-start | bytes 1572872 | tf_op jit(solution)/shard_map/ppermute | solution.py:63
  147.5 39.5 %collective-permute-start.18 = (bf16[2,4,128,256]{3,2,1,0:T(8,128)(2,1)S(1)}, bf16[2,4,128,256]{3,2,1,0:T(8,128)(2,1)S(1)}, u32[]{:S(2)}, u32[]{:S(2)}) collective-permute-start(bf16[2,4,128,256]{3,2,1,0:T(8,128)(2,1)S(1)} %pad_maximum_fusion.2), channel_id=1, source_target_pairs={{0,1},{1,0},{2,3},{3,2},{4,5},{5,4},{6,7},{7,6},{8,9},{9,8},{10,11... | collective-permute-start | bytes 1572872 | tf_op jit(solution)/shard_map/ppermute | solution.py:63
  149.4 25.1 %collective-permute-start.23 = (bf16[4,128,256]{2,1,0:T(8,128)(2,1)S(1)}, bf16[4,128,256]{2,1,0:T(8,128)(2,1)S(1)}, u32[]{:S(2)}, u32[]{:S(2)}) collective-permute-start(bf16[4,128,256]{2,1,0:T(8,128)(2,1)S(1)} %collective-permute-done.21.refs_8_), channel_id=1, source_target_pairs={{0,3},{1,2},{2,1},{3,0},{4,7},{5,6},{6,5},{7,4},{8,11},{9,10},{10,... | collective-permute-start | bytes 786440 | tf_op jit(solution)/shard_map/ppermute | solution.py:63
  151.5 24.9 %collective-permute-start.22 = (bf16[4,128,256]{2,1,0:T(8,128)(2,1)S(1)}, bf16[4,128,256]{2,1,0:T(8,128)(2,1)S(1)}, u32[]{:S(2)}, u32[]{:S(2)}) collective-permute-start(bf16[4,128,256]{2,1,0:T(8,128)(2,1)S(1)} %collective-permute-done.21.refs_8_), channel_id=1, source_target_pairs={{0,1},{1,0},{2,3},{3,2},{4,5},{5,4},{6,7},{7,6},{8,9},{9,8},{10,11... | collective-permute-start | bytes 786440 | tf_op jit(solution)/shard_map/ppermute | solution.py:63
  174.5 31.7 %collective-permute-start.29 = (bf16[2,4,128,256]{3,2,1,0:T(8,128)(2,1)S(1)}, bf16[2,4,128,256]{3,2,1,0:T(8,128)(2,1)S(1)}, u32[]{:S(2)}, u32[]{:S(2)}) collective-permute-start(bf16[2,4,128,256]{3,2,1,0:T(8,128)(2,1)S(1)} %pad_maximum_fusion.3), channel_id=1, source_target_pairs={{0,3},{1,2},{2,1},{3,0},{4,7},{5,6},{6,5},{7,4},{8,11},{9,10},{10,... | collective-permute-start | bytes 1572872 | tf_op jit(solution)/shard_map/ppermute | solution.py:63
  176.5 29.8 %collective-permute-start.28 = (bf16[2,4,128,256]{3,2,1,0:T(8,128)(2,1)S(1)}, bf16[2,4,128,256]{3,2,1,0:T(8,128)(2,1)S(1)}, u32[]{:S(2)}, u32[]{:S(2)}) collective-permute-start(bf16[2,4,128,256]{3,2,1,0:T(8,128)(2,1)S(1)} %pad_maximum_fusion.3), channel_id=1, source_target_pairs={{0,1},{1,0},{2,3},{3,2},{4,5},{5,4},{6,7},{7,6},{8,9},{9,8},{10,11... | collective-permute-start | bytes 1572872 | tf_op jit(solution)/shard_map/ppermute | solution.py:63
  178.6 24.2 %collective-permute-start.30 = (bf16[5,128,256]{2,1,0:T(8,128)(2,1)S(1)}, bf16[5,128,256]{2,1,0:T(8,128)(2,1)S(1)}, u32[]{:S(2)}, u32[]{:S(2)}) collective-permute-start(bf16[5,128,256]{2,1,0:T(8,128)(2,1)S(1)} %pad_maximum_fusion.7), channel_id=1, source_target_pairs={{0,2},{1,3},{2,0},{3,1},{4,6},{5,7},{6,4},{7,5},{8,10},{9,11},{10,... | collective-permute-start | bytes 983048 | tf_op jit(solution)/shard_map/ppermute | solution.py:63
  185.1 21.2 %collective-permute-start.25 = (bf16[5,128,256]{2,1,0:T(8,128)(2,1)S(1)}, bf16[5,128,256]{2,1,0:T(8,128)(2,1)S(1)}, u32[]{:S(2)}, u32[]{:S(2)}) collective-permute-start(bf16[5,128,256]{2,1,0:T(8,128)(2,1)S(1)} %pad_maximum_fusion.6), channel_id=1, source_target_pairs={{0,1},{1,0},{2,3},{3,2},{4,5},{5,4},{6,7},{7,6},{8,9},{9,8},{10,11... | collective-permute-start | bytes 983048 | tf_op jit(solution)/shard_map/ppermute | solution.py:63
  (12 other events, 222.7 us)
